TPU v7x, 256 devices: a whole 4x4x8 slice. The times are simulated.
256 devices in a mesh: dp: 16 (over x, y_hi, core), zero: 16 (over y_lo, z).
Axes of the slice: x: 4, y: 4 (y_hi: 2, y_lo: 2; y = y_hi * 2 + y_lo), z: 8, core: 2. Of those that a mesh axis runs over, the one named last changes fastest.
Arguments:
- picture_embeds: bfloat16 [32768, 1024], P(('dp', 'zero')), may hold values from -4 to 4
- matched_slot: int32 [32768], P(('dp', 'zero')), may hold values from 0 to 2047, as said below
- summary_token_states: bfloat16 [32768, 1024], P(('dp', 'zero')), may hold values from -10 to 10
- feedforward_inner_activations: bfloat16 [32768, 4096], P(('dp', 'zero')), may hold values from -24 to 24
- closing_layernorm_multiplier: float32 [1024], replicated, may hold values from 0.1 to 1.9
- contracting_matrix: bfloat16 [4096, 1024], P('zero'), may hold values from -0.09375 to 0.09375
- sharpness_factor: float32 [1], replicated, may hold values from 3 to 6
- additive_shift_learned: float32 [1], replicated, may hold values from -3 to -1
Outputs:
- image_grad: float32 [32768, 1024], P(('dp', 'zero'))
- hidden_grad: bfloat16 [32768, 4096], P(('dp', 'zero'))
- down_grad: float32 [4096, 1024], P('zero', 'dp')
Inputs may be any that keep to these rules, and one draw needn't show every extreme that they name: `matched_slot`: within the 2048 images of one zero index every position 0 to 2047 is named exactly once.
All inputs are finite; a program needn't handle non-finite values.
Results may differ from a plain program's by a relative error of at most 0.005.
Values may be sent and summed in bfloat16 or wider, within the bound.
A program may use at most 128 MiB of HBM per device.

v0:
```python
import jax
import jax.numpy as jnp
from jax import lax
from jax.sharding import PartitionSpec as P


def unit_rows(values):
    return values * lax.rsqrt(jnp.sum(values * values, axis=1, keepdims=True) + 1e-06)


def text_embed(features, closing_layernorm_multiplier):
    center = features - jnp.mean(features, axis=1, keepdims=True)
    spread = jnp.mean(center * center, axis=1, keepdims=True)
    return unit_rows(center * lax.rsqrt(spread + 1e-05) * closing_layernorm_multiplier)


def sigmoid_weights(scores, labels):
    return (-labels * jax.nn.sigmoid(-labels * scores)).astype(jnp.bfloat16)


def shards(
    picture_embeds,
    matched_slot,
    summary_token_states,
    feedforward_inner_activations,
    closing_layernorm_multiplier,
    contracting_matrix,
    sharpness_factor,
    additive_shift_learned,
):
    similarity_multiplier = sharpness_factor[0]
    shift_value = additive_shift_learned[0]
    local_rows, width = picture_embeds.shape
    dp_size = lax.axis_size("dp")
    zero_size = lax.axis_size("zero")
    dp_place = lax.axis_index("dp")
    own_start = dp_place * local_rows
    transpose_route = [
        (a * zero_size + b, b * zero_size + a) for a in range(dp_size) for b in range(zero_size)
    ]
    ffa_cols = lax.all_to_all(
        feedforward_inner_activations, "dp", split_axis=1, concat_axis=0, tiled=True
    )
    weight_block = lax.ppermute(contracting_matrix, ("dp", "zero"), transpose_route)
    digits = jnp.zeros((local_rows, 128), jnp.bfloat16)
    digits = digits.at[:, 0].set((matched_slot // 256).astype(jnp.bfloat16))
    digits = digits.at[:, 1].set((matched_slot % 256).astype(jnp.bfloat16))
    both = jnp.concatenate([picture_embeds, summary_token_states, digits], axis=1)
    both_g = lax.all_gather(both, "dp", axis=0, tiled=True)
    ffa_cols, weight_block, both_g = lax.optimization_barrier((ffa_cols, weight_block, both_g))
    slot_g = both_g[:, 2 * width].astype(jnp.int32) * 256 + both_g[:, 2 * width + 1].astype(
        jnp.int32
    )
    image_b_g = unit_rows(both_g[:, :width].astype(jnp.float32)).astype(jnp.bfloat16)
    caption_g, caption_back = jax.vjp(
        lambda feats: text_embed(feats, closing_layernorm_multiplier),
        both_g[:, width : 2 * width].astype(jnp.float32),
    )
    caption_b_g = caption_g.astype(jnp.bfloat16)
    group_rows = caption_b_g.shape[0]
    unit_image, image_back = jax.vjp(unit_rows, picture_embeds.astype(jnp.float32))
    scores = (
        similarity_multiplier
        * lax.dot_general(
            image_b_g, caption_b_g, (((1,), (1,)), ((), ())), preferred_element_type=jnp.float32
        )
        + shift_value
    )
    places = jnp.arange(group_rows, dtype=jnp.int32)
    labels = jnp.where(slot_g[:, None] == places[None, :], 1.0, -1.0)
    weights = sigmoid_weights(scores, labels)
    own_weights = lax.dynamic_slice_in_dim(weights, own_start, local_rows, axis=0)
    image_term = similarity_multiplier * jnp.dot(
        own_weights, caption_b_g, preferred_element_type=jnp.float32
    )
    caption_term = similarity_multiplier * lax.dot_general(
        weights, image_b_g, (((0,), (0,)), ((), ())), preferred_element_type=jnp.float32
    )
    image_grad = image_back(image_term)[0]
    upstream_g = caption_back(caption_term)[0].astype(jnp.bfloat16)
    hidden_part = lax.dot_general(
        upstream_g, weight_block, (((1,), (1,)), ((), ())), preferred_element_type=jnp.float32
    ).astype(jnp.bfloat16)
    hidden_grad = lax.all_to_all(hidden_part, "dp", split_axis=0, concat_axis=1, tiled=True)
    group_sum = lax.dot_general(
        ffa_cols, upstream_g, (((0,), (0,)), ((), ())), preferred_element_type=jnp.float32
    )
    down_parts = lax.all_to_all(group_sum, "zero", split_axis=1, concat_axis=0, tiled=True)
    down_block = jnp.sum(down_parts.reshape((zero_size,) + (group_sum.shape[0], -1)), axis=0)
    down_grad = lax.ppermute(down_block, ("dp", "zero"), transpose_route)
    return (image_grad, hidden_grad, down_grad)


def solution(mesh):
    placed = (
        P(("dp", "zero"), None),
        P(("dp", "zero")),
        P(("dp", "zero"), None),
        P(("dp", "zero"), None),
        P(),
        P("zero", None),
        P(),
        P(),
    )
    return jax.shard_map(
        shards,
        mesh=mesh,
        in_specs=placed,
        out_specs=(P(("dp", "zero"), None), P(("dp", "zero"), None), P("zero", "dp")),
        check_vma=False,
    )
```

profile of v0, /device:TPU:1, one launch (start us, length us, event | category | flops | bytes accessed | tf_op | source)
XLA Modules:
  0.0 254.7 jit_solution(212489842081570415)
XLA Ops:
  7.2 0.0 all-gather.2.cloned.1.call-start
  7.2 0.6 compare_reduce_fusion.1
  7.8 0.6 compare_reduce_fusion
  8.5 1.1 copy.21
  9.6 0.0 copy-start.3
  9.6 1.1 copy.20
  10.8 2.0 fusion.26
  12.8 0.9 pad_maximum_fusion
  13.7 0.0 all-gather.2.cloned.1.call-update
  13.7 2.3 copy.18
  16.0 8.4 %all-to-all-start = ((bf16[128,16,256]{0,2,1:T(8,128)(2,1)}), bf16[128,16,256]{0,2,1:T(8,128)(2,1)S(1)}, u32[]{:S(2)}, u32[]{:S(2)}) async-start(bf16[128,16,256]{0,2,1:T(8,128)(2,1)} %bitcast.1), calls=%async_computation | async-start | bytes 2097152 | tf_op jit(solution)/shard_map/all_to_all | solution.py:41
  24.4 3.5 %collective-permute-start = (bf16[256,1024]{1,0:T(8,128)(2,1)}, bf16[256,1024]{1,0:T(8,128)(2,1)S(1)}, u32[]{:S(2)}, u32[]{:S(2)}) collective-permute-start(bf16[256,1024]{1,0:T(8,128)(2,1)} %param.17), channel_id=1, source_target_pairs={{0,0},{1,16},{2,32},{3,48},{4,64},{5,80},{6,96},{7,112},{8,128},{9... | collective-permute-start | bytes 1572872 | tf_op jit(solution)/shard_map/ppermute | solution.py:44
  29.3 34.6 %all-to-all-done = bf16[128,16,256]{0,2,1:T(8,128)(2,1)S(1)} async-done(((bf16[128,16,256]{0,2,1:T(8,128)(2,1)}), bf16[128,16,256]{0,2,1:T(8,128)(2,1)S(1)}, u32[]{:S(2)}, u32[]{:S(2)}) %all-to-all-start) | async-done | bytes 1048608 | tf_op jit(solution)/shard_map/all_to_all | solution.py:41
  63.8 0.5 copy.19
  64.4 0.0 collective-permute-done
  64.4 69.7 %all-gather.2.cloned.1.call-done = bf16[2048,2176]{0,1:T(8,128)(2,1)} async-done(((bf16[128,2176]{0,1:T(8,128)(2,1)}), bf16[2048,2176]{0,1:T(8,128)(2,1)}) %all-gather.2.cloned.1.call-update) | async-done | bytes 8912912 | tf_op jit(solution)/shard_map/all_gather | solution.py:49
  134.1 0.0 copy-start
  134.1 3.0 %convert_reduce_fusion = f32[2048]{0:T(1024)S(1)} fusion(bf16[2048,2176]{0,1:T(8,128)(2,1)} %all-gather.2.cloned.1.call-done), kind=kLoop, calls=%fused_computation.5 | loop fusion | flops 4192256 | bytes 4202496 | tf_op jit(solution)/shard_map/jvp()/reduce_sum | solution.py:12
  137.1 1.3 convert_add_fusion
  138.4 3.3 %fusion.6 = f32[2048]{0:T(1024)S(1)} fusion(f32[2048]{0:T(1024)S(1)} %broadcast_multiply_fusion, bf16[2048,2176]{0,1:T(8,128)(2,1)} %all-gather.2.cloned.1.call-done), kind=kLoop, calls=%fused_computation.14 | loop fusion | flops 8386560 | bytes 4210688 | tf_op jit(solution)/shard_map/jvp()/reduce_sum | solution.py:13
  141.7 0.0 copy-done.3
  141.7 5.1 %fusion.12 = (f32[2048]{0:T(1024)S(1)}, f32[2048]{0:T(1024)S(1)}) fusion(f32[1024]{0:T(1024)S(1)} %copy-done.3, f32[2048]{0:T(1024)S(1)} %fusion.24, f32[2048]{0:T(1024)S(1)} %broadcast_multiply_fusion, bf16[2048,2176]{0,1:T(8,128)(2,1)} %all-gather.2.cloned.1.call-done), kind=kLoop, calls=%fused_computation.20 | loop fusion | flops 18870272 | bytes 8425472 | tf_op jit(solution)/shard_map/jvp()/reduce_sum | solution.py:8
  146.9 0.0 copy-done
  146.9 18.2 %multiply_convert_fusion = bf16[2048,2048]{1,0:T(8,128)(2,1)} fusion(f32[]{:T(128)} %bitcast.23, f32[]{:T(128)} %bitcast.19, s32[2048]{0:T(1024)S(1)} %bitcast.28, f32[2048]{0:T(1024)S(1)} %get-tuple-element.46, bf16[2048,2176]{0,1:T(8,128)(2,1)S(1)} %copy-done, f32[2048]{0:T(1024)S(1)} %get-tuple-element.47, f32[1024]{0:T(1024)S(1)} %copy-done.3, ...), kind=kOutput, calls=%fused_computation | convolution fusion | flops 8654946304 | bytes 16822280 | tf_op jit(solution)/shard_map/dot_general | solution.py:64
  165.1 11.9 %fusion.14 = (f32[2048]{0:T(1024)S(1)}, f32[2048,1024]{0,1:T(8,128)S(1)}) fusion(f32[]{:T(128)} %bitcast.22, f32[1024]{0:T(1024)S(1)} %copy-done.3, f32[2048]{0:T(1024)S(1)} %fusion.24, f32[2048]{0:T(1024)S(1)} %broadcast_multiply_fusion, bf16[2048,2176]{0,1:T(8,128)(2,1)S(1)} %copy-done, bf16[2048,2048]{1,0:T(8,128)(2,1)} %multiply_convert_fusion, ...), kind=kOutput, calls=%fused_computation.22 | convolution fusion | flops 8610904064 | bytes 25202692 | tf_op jit(solution)/shard_map/dot_general | solution.py:76
  177.0 3.9 %fusion.15 = f32[2048]{0:T(1024)S(1)} fusion(f32[2048,1024]{0,1:T(8,128)S(1)} %get-tuple-element.45, f32[2048]{0:T(1024)S(1)} %multiply_multiply_fusion.1, f32[]{:T(128)} %bitcast.21, f32[2048]{0:T(1024)S(1)} %get-tuple-element.47, f32[1024]{0:T(1024)S(1)} %copy-done.3, f32[2048]{0:T(1024)S(1)} %fusion.24, f32[2048]{0:T(1024)S(1)} %broadcast_multiply_fusion, ...), kind=kLoop, calls=%fused_computation.23 | loop fusion | flops 25163776 | bytes 12627972 | tf_op jit(solution)/shard_map/transpose(jvp())/reduce_sum | solution.py:14
  180.9 4.6 %fusion.31 = (f32[2048]{0:T(1024)S(1)}, f32[2048,1024]{0,1:T(8,128)S(1)}) fusion(f32[2048]{0:T(1024)S(1)} %multiply_multiply_fusion, f32[2048]{0:T(1024)S(1)} %multiply_multiply_fusion.1, f32[1024]{0:T(1024)S(1)} %copy-done.3, f32[2048]{0:T(1024)S(1)} %fusion.24, f32[2048]{0:T(1024)S(1)} %broadcast_multiply_fusion, bf16[2048,2176]{0,1:T(8,128)(2,1)S(1)} %copy-done, ...), kind=kLoop, calls=%fused_computation.63 | loop fusion | flops 31455232 | bytes 21024772 | tf_op jit(solution)/shard_map/transpose(jvp())/reduce_sum | solution.py:12
  185.5 0.0 copy-start.1
  185.6 2.9 %fusion.20 = f32[256,1024]{0,1:T(8,128)} fusion(bf16[2048,256]{1,0:T(8,128)(2,1)S(1)} %bitcast.26, f32[2048,1024]{0,1:T(8,128)S(1)} %get-tuple-element.38, f32[2048]{0:T(1024)S(1)} %negate_multiply_fusion), kind=kOutput, calls=%fused_computation.28 | convolution fusion | flops 1077936128 | bytes 10493952 | tf_op jit(solution)/shard_map/dot_general | solution.py:85
  188.4 0.8 copy-done.1
  189.2 6.9 %all-to-all-start.2 = ((f32[256,16,64]{0,2,1:T(8,128)}), f32[256,16,64]{0,2,1:T(8,128)S(1)}, u32[]{:S(2)}, u32[]{:S(2)}) async-start(f32[256,16,64]{0,2,1:T(8,128)} %bitcast.10), calls=%async_computation.2 | async-start | bytes 2097152 | tf_op jit(solution)/shard_map/all_to_all | solution.py:88
  196.0 0.0 copy-start.2
  196.1 5.8 %convolution_convert_fusion = bf16[2048,256]{1,0:T(8,128)(2,1)} fusion(bf16[256,1024]{1,0:T(8,128)(2,1)S(1)} %collective-permute-done, f32[2048,1024]{0,1:T(8,128)} %copy-done.1, f32[2048]{0:T(1024)S(1)} %negate_multiply_fusion), kind=kOutput, calls=%fused_computation.27 | convolution fusion | flops 1078460416 | bytes 9969664 | tf_op jit(solution)/shard_map/dot_general | solution.py:81
  201.8 19.7 %all-to-all-done.2 = f32[256,16,64]{0,2,1:T(8,128)S(1)} async-done(((f32[256,16,64]{0,2,1:T(8,128)}), f32[256,16,64]{0,2,1:T(8,128)S(1)}, u32[]{:S(2)}, u32[]{:S(2)}) %all-to-all-start.2) | async-done | bytes 1048608 | tf_op jit(solution)/shard_map/all_to_all | solution.py:88
  221.5 7.4 %all-to-all-start.1 = ((bf16[16,128,256]{2,1,0:T(8,128)(2,1)}), bf16[16,128,256]{2,1,0:T(8,128)(2,1)S(1)}, u32[]{:S(2)}, u32[]{:S(2)}) async-start(bf16[16,128,256]{2,1,0:T(8,128)(2,1)} %bitcast.8), calls=%async_computation.1 | async-start | bytes 2097152 | tf_op jit(solution)/shard_map/all_to_all | solution.py:84
  228.9 0.0 copy-done.2
  228.9 4.2 %fusion.21 = (f32[128]{0:T(128)S(1)}, f32[128]{0:T(128)S(1)}, f32[128,1024]{1,0:T(8,128)S(1)}) fusion(bf16[128,1024]{1,0:T(8,128)(2,1)S(1)} %copy-done.2, f32[2048]{0:T(1024)S(1)} %get-tuple-element.47, f32[1024]{0:T(1024)S(1)} %copy-done.3, f32[2048]{0:T(1024)S(1)} %fusion.24, f32[2048]{0:T(1024)S(1)} %broadcast_multiply_fusion, ...), kind=kOutput, calls=%fused_computation.35 | convolution fusion | flops 550240000 | bytes 5535236 | tf_op jit(solution)/shard_map/dot_general | solution.py:73
  233.2 0.1 reduce_sum.115
  233.2 2.7 %collective-permute-start.1 = (f32[256,64]{0,1:T(8,128)S(1)}, f32[256,64]{0,1:T(8,128)S(1)}, u32[]{:S(2)}, u32[]{:S(2)}) collective-permute-start(f32[256,64]{0,1:T(8,128)S(1)} %reduce_sum.115), channel_id=1, source_target_pairs={{0,0},{1,16},{2,32},{3,48},{4,64},{5,80},{6,96},{7,112},{8,128},{9... | collective-permute-start | bytes 196616 | tf_op jit(solution)/shard_map/ppermute | solution.py:90
  236.0 1.0 add_add_fusion.2
  236.9 9.2 %all-to-all-done.1 = bf16[16,128,256]{2,1,0:T(8,128)(2,1)S(1)} async-done(((bf16[16,128,256]{2,1,0:T(8,128)(2,1)}), bf16[16,128,256]{2,1,0:T(8,128)(2,1)S(1)}, u32[]{:S(2)}, u32[]{:S(2)}) %all-to-all-start.1) | async-done | bytes 1048608 | tf_op jit(solution)/shard_map/all_to_all | solution.py:84
  246.1 1.1 copy.25
  247.2 0.0 collective-permute-done.1
  247.2 0.6 copy.30
  (9 shorter events, 0.1 us)
Async XLA Ops:
  7.2 126.9 %all-gather.2.cloned.1.call-start = ((), (), s32[]{:S(2)}) async-start(), calls=%async_computation.3 | async-start | bytes 9469952 | tf_op jit(solution)/shard_map/all_gather | solution.py:49
  9.6 132.1 %copy-start.3 = (f32[1024]{0:T(1024)S(1)}, f32[1024]{0:T(1024)}, u32[]{:S(2)}) copy-start(f32[1024]{0:T(1024)} %param.16) | copy-start | bytes 12292
  16.0 47.8 %all-to-all-start = ((bf16[128,16,256]{0,2,1:T(8,128)(2,1)}), bf16[128,16,256]{0,2,1:T(8,128)(2,1)S(1)}, u32[]{:S(2)}, u32[]{:S(2)}) async-start(bf16[128,16,256]{0,2,1:T(8,128)(2,1)} %bitcast.1), calls=%async_computation | async-start | bytes 2097152 | tf_op jit(solution)/shard_map/all_to_all | solution.py:41
  24.4 39.9 %collective-permute-start = (bf16[256,1024]{1,0:T(8,128)(2,1)}, bf16[256,1024]{1,0:T(8,128)(2,1)S(1)}, u32[]{:S(2)}, u32[]{:S(2)}) collective-permute-start(bf16[256,1024]{1,0:T(8,128)(2,1)} %param.17), channel_id=1, source_target_pairs={{0,0},{1,16},{2,32},{3,48},{4,64},{5,80},{6,96},{7,112},{8,128},{9... | collective-permute-start | bytes 1572872 | tf_op jit(solution)/shard_map/ppermute | solution.py:44
  134.1 12.8 %copy-start = (bf16[2048,2176]{0,1:T(8,128)(2,1)S(1)}, bf16[2048,2176]{0,1:T(8,128)(2,1)}, u32[]{:S(2)}) copy-start(bf16[2048,2176]{0,1:T(8,128)(2,1)} %all-gather.2.cloned.1.call-done) | copy-start | bytes 26738692
  185.5 3.6 %copy-start.1 = (f32[2048,1024]{0,1:T(8,128)}, f32[2048,1024]{0,1:T(8,128)S(1)}, u32[]{:S(2)}) copy-start(f32[2048,1024]{0,1:T(8,128)S(1)} %get-tuple-element.38) | copy-start | bytes 25165828
  189.2 32.3 %all-to-all-start.2 = ((f32[256,16,64]{0,2,1:T(8,128)}), f32[256,16,64]{0,2,1:T(8,128)S(1)}, u32[]{:S(2)}, u32[]{:S(2)}) async-start(f32[256,16,64]{0,2,1:T(8,128)} %bitcast.10), calls=%async_computation.2 | async-start | bytes 2097152 | tf_op jit(solution)/shard_map/all_to_all | solution.py:88
  196.0 32.9 %copy-start.2 = (bf16[128,1024]{1,0:T(8,128)(2,1)S(1)}, bf16[128,1024]{1,0:T(8,128)(2,1)}, u32[]{:S(2)}) copy-start(bf16[128,1024]{1,0:T(8,128)(2,1)} %param.12) | copy-start | bytes 786436
  221.5 24.6 %all-to-all-start.1 = ((bf16[16,128,256]{2,1,0:T(8,128)(2,1)}), bf16[16,128,256]{2,1,0:T(8,128)(2,1)S(1)}, u32[]{:S(2)}, u32[]{:S(2)}) async-start(bf16[16,128,256]{2,1,0:T(8,128)(2,1)} %bitcast.8), calls=%async_computation.1 | async-start | bytes 2097152 | tf_op jit(solution)/shard_map/all_to_all | solution.py:84
  233.2 14.0 %collective-permute-start.1 = (f32[256,64]{0,1:T(8,128)S(1)}, f32[256,64]{0,1:T(8,128)S(1)}, u32[]{:S(2)}, u32[]{:S(2)}) collective-permute-start(f32[256,64]{0,1:T(8,128)S(1)} %reduce_sum.115), channel_id=1, source_target_pairs={{0,0},{1,16},{2,32},{3,48},{4,64},{5,80},{6,96},{7,112},{8,128},{9... | collective-permute-start | bytes 196616 | tf_op jit(solution)/shard_map/ppermute | solution.py:90
Sparse Core Ops, SparseCore 0:
  13.8 120.1 all-gather.1
where the time goes:
time: 255 us
  waiting for transfers between devices  133 us (52%)
  matrix products  42.9 us (17%)
  starting transfers between devices  29 us (11%)
  other arithmetic  26.4 us (10%)
  between operations  15.5 us (6%)
  local copies, waits for them, and re-layouts  7.57 us (3%)
    all_gather x1, waiting for transfers between devices, shards(): both_g = lax.all_gather(both, 'dp', axis=0, tiled=True)  69.7 us
    all_to_all x1, waiting for transfers between devices, shards(): lax.all_to_all(feedforward_inner_activations, 'dp', split_axis=1, concat_...  34.6 us
    all_to_all x1, waiting for transfers between devices, shards(): lax.all_to_all(group_sum, 'zero', split_axis=1, concat_axis=0, tiled=True)  19.7 us
    dot_general x1, matrix products, shards(): lax.dot_general(image_b_g, caption_b_g, (((1,), (1,)), ((), ())), preferr...  18.2 us
    dot_general x1, matrix products, shards(): lax.dot_general(weights, image_b_g, (((0,), (0,)), ((), ())), preferred_e...  11.9 us
    all_to_all x1, waiting for transfers between devices, shards(): lax.all_to_all(hidden_part, 'dp', split_axis=0, concat_axis=1, tiled=True)  9.2 us
    all_to_all x1, starting transfers between devices, shards(): lax.all_to_all(feedforward_inner_activations, 'dp', split_axis=1, concat_...  8.45 us
    reduce_sum x2, other arithmetic, text_embed(): center = features - jnp.mean(features, axis=1, keepdims=True)  7.6 us
  transfers between devices with their start and end apart: 6, of which 4 were waited for; matrix products, arithmetic and copies ran while one was open for 6% of the time, Pallas kernels for 0%

commit v1 on v0

--- a/solution.py
+++ b/solution.py
@@ -85,7 +85,12 @@
     group_sum = lax.dot_general(
         ffa_cols, upstream_g, (((0,), (0,)), ((), ())), preferred_element_type=jnp.float32
     )
-    down_parts = lax.all_to_all(group_sum, "zero", split_axis=1, concat_axis=0, tiled=True)
+    down_parts = jnp.concatenate(
+        jax.lax.all_to_all(
+            jnp.stack(jnp.split(group_sum, jax.lax.psum(1, "zero"), 1), 0), "zero", 0, 0
+        ),
+        0,
+    )
     down_block = jnp.sum(down_parts.reshape((zero_size,) + (group_sum.shape[0], -1)), axis=0)
     down_grad = lax.ppermute(down_block, ("dp", "zero"), transpose_route)
     return (image_grad, hidden_grad, down_grad)

time: 255 us -> 262 us (1.027); the launches traced: 255 us -> 258 us
  local copies, waits for them, and re-layouts: 7.57 us -> 12.7 us
    unnamed x12 -> x28, local copies, waits for them, and re-layouts: 5.93 us -> 9.38 us
where the time goes in v1:
time: 262 us; the launch traced here: 258 us
  waiting for transfers between devices  133 us (51%)
  matrix products  41.4 us (16%)
  starting transfers between devices  29.1 us (11%)
  other arithmetic  26.4 us (10%)
  between operations  15.7 us (6%)
  local copies, waits for them, and re-layouts  12.7 us (5%)
    all_gather x1, waiting for transfers between devices, shards(): both_g = lax.all_gather(both, 'dp', axis=0, tiled=True)  69.7 us
    all_to_all x1, waiting for transfers between devices, shards(): lax.all_to_all(feedforward_inner_activations, 'dp', split_axis=1, concat_...  34.6 us
    all_to_all x1, waiting for transfers between devices, shards(): jax.lax.all_to_all(jnp.stack(jnp.split(group_sum, jax.lax.psum(1, 'zero')...  19.6 us
    dot_general x1, matrix products, shards(): lax.dot_general(image_b_g, caption_b_g, (((1,), (1,)), ((), ())), preferr...  18.2 us
    dot_general x1, matrix products, shards(): lax.dot_general(weights, image_b_g, (((0,), (0,)), ((), ())), preferred_e...  11.9 us
    unnamed x28, local copies, waits for them, and re-layouts  9.38 us
    all_to_all x1, waiting for transfers between devices, shards(): lax.all_to_all(hidden_part, 'dp', split_axis=0, concat_axis=1, tiled=True)  9.11 us
    all_to_all x1, starting transfers between devices, shards(): lax.all_to_all(feedforward_inner_activations, 'dp', split_axis=1, concat_...  8.45 us
  transfers between devices with their start and end apart: 6, of which 4 were waited for; matrix products, arithmetic and copies ran while one was open for 6% of the time, Pallas kernels for 0%

profile of v1, /device:TPU:1, one launch (start us, length us, event | category | flops | bytes accessed | tf_op | source)
XLA Modules:
  0.0 258.3 jit_solution(12395940702288194713)
XLA Ops:
  7.2 0.0 all-gather.2.cloned.1.call-start
  7.2 0.6 compare_reduce_fusion.1
  7.8 0.6 compare_reduce_fusion
  8.5 1.1 copy.25
  9.6 0.0 copy-start.3
  9.6 1.1 copy.24
  10.8 2.0 fusion.42
  12.8 0.9 pad_maximum_fusion
  13.7 0.0 all-gather.2.cloned.1.call-update
  13.7 2.3 copy.22
  16.0 8.4 %all-to-all-start = ((bf16[128,16,256]{0,2,1:T(8,128)(2,1)}), bf16[128,16,256]{0,2,1:T(8,128)(2,1)S(1)}, u32[]{:S(2)}, u32[]{:S(2)}) async-start(bf16[128,16,256]{0,2,1:T(8,128)(2,1)} %bitcast.1), calls=%async_computation | async-start | bytes 2097152 | tf_op jit(solution)/shard_map/all_to_all | solution.py:41
  24.4 3.5 %collective-permute-start = (bf16[256,1024]{1,0:T(8,128)(2,1)}, bf16[256,1024]{1,0:T(8,128)(2,1)S(1)}, u32[]{:S(2)}, u32[]{:S(2)}) collective-permute-start(bf16[256,1024]{1,0:T(8,128)(2,1)} %param.17), channel_id=1, source_target_pairs={{0,0},{1,16},{2,32},{3,48},{4,64},{5,80},{6,96},{7,112},{8,128},{9... | collective-permute-start | bytes 1572872 | tf_op jit(solution)/shard_map/ppermute | solution.py:44
  29.3 34.6 %all-to-all-done = bf16[128,16,256]{0,2,1:T(8,128)(2,1)S(1)} async-done(((bf16[128,16,256]{0,2,1:T(8,128)(2,1)}), bf16[128,16,256]{0,2,1:T(8,128)(2,1)S(1)}, u32[]{:S(2)}, u32[]{:S(2)}) %all-to-all-start) | async-done | bytes 1048608 | tf_op jit(solution)/shard_map/all_to_all | solution.py:41
  63.8 0.5 copy.23
  64.3 0.0 collective-permute-done
  64.3 69.7 %all-gather.2.cloned.1.call-done = bf16[2048,2176]{0,1:T(8,128)(2,1)} async-done(((bf16[128,2176]{0,1:T(8,128)(2,1)}), bf16[2048,2176]{0,1:T(8,128)(2,1)}) %all-gather.2.cloned.1.call-update) | async-done | bytes 8912912 | tf_op jit(solution)/shard_map/all_gather | solution.py:49
  134.1 0.0 copy-start
  134.1 3.0 %convert_reduce_fusion = f32[2048]{0:T(1024)S(1)} fusion(bf16[2048,2176]{0,1:T(8,128)(2,1)} %all-gather.2.cloned.1.call-done), kind=kLoop, calls=%fused_computation.5 | loop fusion | flops 4192256 | bytes 4202496 | tf_op jit(solution)/shard_map/jvp()/reduce_sum | solution.py:12
  137.1 1.3 convert_add_fusion
  138.4 3.3 %fusion.6 = f32[2048]{0:T(1024)S(1)} fusion(f32[2048]{0:T(1024)S(1)} %broadcast_multiply_fusion, bf16[2048,2176]{0,1:T(8,128)(2,1)} %all-gather.2.cloned.1.call-done), kind=kLoop, calls=%fused_computation.14 | loop fusion | flops 8386560 | bytes 4210688 | tf_op jit(solution)/shard_map/jvp()/reduce_sum | solution.py:13
  141.7 0.0 copy-done.3
  141.7 5.1 %fusion.12 = (f32[2048]{0:T(1024)S(1)}, f32[2048]{0:T(1024)S(1)}) fusion(f32[1024]{0:T(1024)S(1)} %copy-done.3, f32[2048]{0:T(1024)S(1)} %fusion.40, f32[2048]{0:T(1024)S(1)} %broadcast_multiply_fusion, bf16[2048,2176]{0,1:T(8,128)(2,1)} %all-gather.2.cloned.1.call-done), kind=kLoop, calls=%fused_computation.20 | loop fusion | flops 18870272 | bytes 8425472 | tf_op jit(solution)/shard_map/jvp()/reduce_sum | solution.py:8
  146.8 0.0 copy-done
  146.9 18.2 %multiply_convert_fusion = bf16[2048,2048]{1,0:T(8,128)(2,1)} fusion(f32[]{:T(128)} %bitcast.86, f32[]{:T(128)} %bitcast.82, s32[2048]{0:T(1024)S(1)} %bitcast.91, f32[2048]{0:T(1024)S(1)} %get-tuple-element.49, bf16[2048,2176]{0,1:T(8,128)(2,1)S(1)} %copy-done, f32[2048]{0:T(1024)S(1)} %get-tuple-element.50, f32[1024]{0:T(1024)S(1)} %copy-done.3, ...), kind=kOutput, calls=%fused_computation | convolution fusion | flops 8654946304 | bytes 16822280 | tf_op jit(solution)/shard_map/dot_general | solution.py:64
  165.1 11.9 %fusion.14 = (f32[2048]{0:T(1024)S(1)}, f32[2048,1024]{0,1:T(8,128)S(1)}) fusion(f32[]{:T(128)} %bitcast.85, f32[1024]{0:T(1024)S(1)} %copy-done.3, f32[2048]{0:T(1024)S(1)} %fusion.40, f32[2048]{0:T(1024)S(1)} %broadcast_multiply_fusion, bf16[2048,2176]{0,1:T(8,128)(2,1)S(1)} %copy-done, bf16[2048,2048]{1,0:T(8,128)(2,1)} %multiply_convert_fusion, ...), kind=kOutput, calls=%fused_computation.22 | convolution fusion | flops 8610904064 | bytes 25202692 | tf_op jit(solution)/shard_map/dot_general | solution.py:76
  177.0 3.9 %fusion.15 = f32[2048]{0:T(1024)S(1)} fusion(f32[2048,1024]{0,1:T(8,128)S(1)} %get-tuple-element.48, f32[2048]{0:T(1024)S(1)} %multiply_multiply_fusion.1, f32[]{:T(128)} %bitcast.84, f32[2048]{0:T(1024)S(1)} %get-tuple-element.50, f32[1024]{0:T(1024)S(1)} %copy-done.3, f32[2048]{0:T(1024)S(1)} %fusion.40, f32[2048]{0:T(1024)S(1)} %broadcast_multiply_fusion, ...), kind=kLoop, calls=%fused_computation.23 | loop fusion | flops 25163776 | bytes 12627972 | tf_op jit(solution)/shard_map/transpose(jvp())/reduce_sum | solution.py:14
  180.9 4.6 %fusion.47 = (f32[2048]{0:T(1024)S(1)}, f32[2048,1024]{0,1:T(8,128)S(1)}) fusion(f32[2048]{0:T(1024)S(1)} %multiply_multiply_fusion, f32[2048]{0:T(1024)S(1)} %multiply_multiply_fusion.1, f32[1024]{0:T(1024)S(1)} %copy-done.3, f32[2048]{0:T(1024)S(1)} %fusion.40, f32[2048]{0:T(1024)S(1)} %broadcast_multiply_fusion, bf16[2048,2176]{0,1:T(8,128)(2,1)S(1)} %copy-done, ...), kind=kLoop, calls=%fused_computation.95 | loop fusion | flops 31455232 | bytes 21024772 | tf_op jit(solution)/shard_map/transpose(jvp())/reduce_sum | solution.py:12
  185.5 0.0 copy-start.1
  185.5 3.2 %copy-done.1 = f32[2048,1024]{0,1:T(8,128)} copy-done((f32[2048,1024]{0,1:T(8,128)}, f32[2048,1024]{0,1:T(8,128)S(1)}, u32[]{:S(2)}) %copy-start.1) | copy-done | bytes 8388632
  188.8 1.3 fusion.20
  190.1 0.1 fusion.38
  190.3 0.1 fusion.36
  190.4 0.1 fusion.34
  190.5 0.1 fusion.32
  190.7 0.1 fusion.30
  190.8 0.1 fusion.28
  190.9 0.1 fusion.26
  191.0 0.1 fusion.24
  191.1 1.6 copy.27
  192.8 6.9 %all-to-all-start.2 = ((f32[16,256,64]{1,2,0:T(8,128)}), f32[16,256,64]{1,2,0:T(8,128)S(1)}, u32[]{:S(2)}, u32[]{:S(2)}) async-start(f32[16,256,64]{1,2,0:T(8,128)} %copy.27), calls=%async_computation.2 | async-start | bytes 2097152 | tf_op jit(solution)/shard_map/all_to_all | solution.py:89
  199.6 0.0 copy-start.2
  199.6 5.8 %convolution_convert_fusion = bf16[2048,256]{1,0:T(8,128)(2,1)} fusion(bf16[256,1024]{1,0:T(8,128)(2,1)S(1)} %collective-permute-done, f32[2048,1024]{0,1:T(8,128)} %copy-done.1, f32[2048]{0:T(1024)S(1)} %negate_multiply_fusion), kind=kOutput, calls=%fused_computation.27 | convolution fusion | flops 1078460416 | bytes 9969664 | tf_op jit(solution)/shard_map/dot_general | solution.py:81
  205.4 19.6 %all-to-all-done.2 = f32[16,256,64]{1,2,0:T(8,128)S(1)} async-done(((f32[16,256,64]{1,2,0:T(8,128)}), f32[16,256,64]{1,2,0:T(8,128)S(1)}, u32[]{:S(2)}, u32[]{:S(2)}) %all-to-all-start.2) | async-done | bytes 1048608 | tf_op jit(solution)/shard_map/all_to_all | solution.py:89
  225.0 7.5 %all-to-all-start.1 = ((bf16[16,128,256]{2,1,0:T(8,128)(2,1)}), bf16[16,128,256]{2,1,0:T(8,128)(2,1)S(1)}, u32[]{:S(2)}, u32[]{:S(2)}) async-start(bf16[16,128,256]{2,1,0:T(8,128)(2,1)} %bitcast.8), calls=%async_computation.1 | async-start | bytes 2097152 | tf_op jit(solution)/shard_map/all_to_all | solution.py:84
  232.5 0.0 copy-done.2
  232.5 4.2 %fusion.21 = (f32[128]{0:T(128)S(1)}, f32[128]{0:T(128)S(1)}, f32[128,1024]{1,0:T(8,128)S(1)}) fusion(bf16[128,1024]{1,0:T(8,128)(2,1)S(1)} %copy-done.2, f32[2048]{0:T(1024)S(1)} %get-tuple-element.50, f32[1024]{0:T(1024)S(1)} %copy-done.3, f32[2048]{0:T(1024)S(1)} %fusion.40, f32[2048]{0:T(1024)S(1)} %broadcast_multiply_fusion, ...), kind=kOutput, calls=%fused_computation.35 | convolution fusion | flops 550240000 | bytes 5535236 | tf_op jit(solution)/shard_map/dot_general | solution.py:73
  236.7 0.1 reduce_sum.115
  236.8 0.1 copy.30
  236.9 2.7 %collective-permute-start.1 = (f32[256,64]{1,0:T(8,128)S(1)}, f32[256,64]{1,0:T(8,128)S(1)}, u32[]{:S(2)}, u32[]{:S(2)}) collective-permute-start(f32[256,64]{1,0:T(8,128)S(1)} %copy.30), channel_id=1, source_target_pairs={{0,0},{1,16},{2,32},{3,48},{4,64},{5,80},{6,96},{7,112},{8,128},{9... | collective-permute-start | bytes 196616 | tf_op jit(solution)/shard_map/ppermute | solution.py:95
  239.6 0.9 add_add_fusion.2
  240.6 9.1 %all-to-all-done.1 = bf16[16,128,256]{2,1,0:T(8,128)(2,1)S(1)} async-done(((bf16[16,128,256]{2,1,0:T(8,128)(2,1)}), bf16[16,128,256]{2,1,0:T(8,128)(2,1)S(1)}, u32[]{:S(2)}, u32[]{:S(2)}) %all-to-all-start.1) | async-done | bytes 1048608 | tf_op jit(solution)/shard_map/all_to_all | solution.py:84
  249.7 1.1 copy.31
  250.8 0.0 collective-permute-done.1
  250.8 0.7 copy.29
  (17 shorter events, 0.3 us)
Async XLA Ops:
  7.2 126.9 %all-gather.2.cloned.1.call-start = ((), (), s32[]{:S(2)}) async-start(), calls=%async_computation.3 | async-start | bytes 9469952 | tf_op jit(solution)/shard_map/all_gather | solution.py:49
  9.6 132.1 %copy-start.3 = (f32[1024]{0:T(1024)S(1)}, f32[1024]{0:T(1024)}, u32[]{:S(2)}) copy-start(f32[1024]{0:T(1024)} %param.16) | copy-start | bytes 12292
  16.0 47.8 %all-to-all-start = ((bf16[128,16,256]{0,2,1:T(8,128)(2,1)}), bf16[128,16,256]{0,2,1:T(8,128)(2,1)S(1)}, u32[]{:S(2)}, u32[]{:S(2)}) async-start(bf16[128,16,256]{0,2,1:T(8,128)(2,1)} %bitcast.1), calls=%async_computation | async-start | bytes 2097152 | tf_op jit(solution)/shard_map/all_to_all | solution.py:41
  24.4 39.9 %collective-permute-start = (bf16[256,1024]{1,0:T(8,128)(2,1)}, bf16[256,1024]{1,0:T(8,128)(2,1)S(1)}, u32[]{:S(2)}, u32[]{:S(2)}) collective-permute-start(bf16[256,1024]{1,0:T(8,128)(2,1)} %param.17), channel_id=1, source_target_pairs={{0,0},{1,16},{2,32},{3,48},{4,64},{5,80},{6,96},{7,112},{8,128},{9... | collective-permute-start | bytes 1572872 | tf_op jit(solution)/shard_map/ppermute | solution.py:44
  134.1 12.8 %copy-start = (bf16[2048,2176]{0,1:T(8,128)(2,1)S(1)}, bf16[2048,2176]{0,1:T(8,128)(2,1)}, u32[]{:S(2)}) copy-start(bf16[2048,2176]{0,1:T(8,128)(2,1)} %all-gather.2.cloned.1.call-done) | copy-start | bytes 26738692
  185.5 3.3 %copy-start.1 = (f32[2048,1024]{0,1:T(8,128)}, f32[2048,1024]{0,1:T(8,128)S(1)}, u32[]{:S(2)}) copy-start(f32[2048,1024]{0,1:T(8,128)S(1)} %get-tuple-element.41) | copy-start | bytes 25165828
  192.8 32.3 %all-to-all-start.2 = ((f32[16,256,64]{1,2,0:T(8,128)}), f32[16,256,64]{1,2,0:T(8,128)S(1)}, u32[]{:S(2)}, u32[]{:S(2)}) async-start(f32[16,256,64]{1,2,0:T(8,128)} %copy.27), calls=%async_computation.2 | async-start | bytes 2097152 | tf_op jit(solution)/shard_map/all_to_all | solution.py:89
  199.6 32.9 %copy-start.2 = (bf16[128,1024]{1,0:T(8,128)(2,1)S(1)}, bf16[128,1024]{1,0:T(8,128)(2,1)}, u32[]{:S(2)}) copy-start(bf16[128,1024]{1,0:T(8,128)(2,1)} %param.12) | copy-start | bytes 786436
  225.0 24.7 %all-to-all-start.1 = ((bf16[16,128,256]{2,1,0:T(8,128)(2,1)}), bf16[16,128,256]{2,1,0:T(8,128)(2,1)S(1)}, u32[]{:S(2)}, u32[]{:S(2)}) async-start(bf16[16,128,256]{2,1,0:T(8,128)(2,1)} %bitcast.8), calls=%async_computation.1 | async-start | bytes 2097152 | tf_op jit(solution)/shard_map/all_to_all | solution.py:84
  236.9 13.9 %collective-permute-start.1 = (f32[256,64]{1,0:T(8,128)S(1)}, f32[256,64]{1,0:T(8,128)S(1)}, u32[]{:S(2)}, u32[]{:S(2)}) collective-permute-start(f32[256,64]{1,0:T(8,128)S(1)} %copy.30), channel_id=1, source_target_pairs={{0,0},{1,16},{2,32},{3,48},{4,64},{5,80},{6,96},{7,112},{8,128},{9... | collective-permute-start | bytes 196616 | tf_op jit(solution)/shard_map/ppermute | solution.py:95
Sparse Core Ops, SparseCore 0:
  13.8 120.1 all-gather.1
